TPU v7x, 128 devices: a whole 4x4x4 slice. The times are simulated.
128 devices in a mesh: inp: 8 (over z, x_hi), tm: 8 (over x_lo, y), bl: 2 (over core).
Axes of the slice: x: 4 (x_hi: 2, x_lo: 2; x = x_hi * 2 + x_lo), y: 4, z: 4, core: 2. Of those that a mesh axis runs over, the one named last changes fastest.
Arguments:
- voltages: int32 [1024, 524288], P(('inp', 'bl'), 'tm'), may hold values from -16 to 14, as said below
- taps: float32 [4, 16384], replicated, may hold values from -3 to 3
- flags: int32 [1024], P(('inp', 'bl')), may hold values 0 or 1
Outputs:
- visibilities: float32 [2, 128, 8, 128, 1024], P(None, ('inp', 'tm'), None, 'bl')
Inputs may be any that keep to these rules, and one draw needn't show every extreme that they name: `voltages`: int8-valued digitized samples, each input's stream in time order.
All inputs are finite; a program needn't handle non-finite values. No bound on the sum of `flags` on one device may be relied on, other than what follows from the above.
Results may differ from a plain program's by a relative error of at most 0.00065.
Values may be sent and summed in bfloat16 or wider, within the bound.
A program may use at most 192 MiB of HBM per device.

v0:
```python
import math
import jax
import jax.numpy as jnp
from jax import lax
from jax.sharding import PartitionSpec as P

CH_AVG = 64


def passed_along(value, axis, steps):
    count = lax.axis_size(axis)
    initial, last = (max(0, -steps), min(count, count - steps))
    return lax.ppermute(value, axis, [(source, source + steps) for source in range(initial, last)])


def cos_sin(height, breadth, period):
    grid = lax.broadcasted_iota(jnp.int32, (height, breadth), 0) * lax.broadcasted_iota(
        jnp.int32, (height, breadth), 1
    )
    angle = (grid % period).astype(jnp.float32) * (2.0 * math.pi / period)
    return (jnp.cos(angle), jnp.sin(angle))


def transform(filtered, length):
    batch = filtered.shape[0]
    first_len = 128
    second_len = length // first_len
    highest = lax.Precision.HIGHEST
    blocks = filtered.reshape(batch, first_len, second_len)
    cos_one, sin_one = cos_sin(first_len, first_len, first_len)
    table_one = jnp.stack([cos_one, -sin_one])
    section_one = jnp.einsum("ykn,mnb->mykb", table_one, blocks, precision=highest)
    cos_twist, sin_twist = cos_sin(first_len, second_len, length)
    real_one = section_one[:, 0]
    imag_one = section_one[:, 1]
    twisted = jnp.stack(
        [real_one * cos_twist + imag_one * sin_twist, imag_one * cos_twist - real_one * sin_twist],
        axis=1,
    )
    cos_two, sin_two = cos_sin(second_len, second_len // 2, second_len)
    table_two = jnp.stack(
        [jnp.stack([cos_two, -sin_two], axis=1), jnp.stack([sin_two, cos_two], axis=1)]
    )
    result = jnp.einsum("mxkb,xbyq->ymqk", twisted, table_two, precision=highest)
    return result.reshape(2, batch, length // 2)


def shards(voltages, taps, flags):
    inputs = voltages.shape[0]
    tap_count = taps.shape[0]
    length = taps.shape[1]
    spectra_dev = voltages.shape[1] // length
    reach = tap_count - 1
    samples = voltages.astype(jnp.float32).reshape(inputs, spectra_dev, length)
    leading = voltages[:, : reach * length].reshape(inputs, reach, length).astype(jnp.bfloat16)
    following = passed_along(leading, "tm", -1)
    extended = jnp.concatenate([samples, following.astype(jnp.float32)], axis=1)
    filtered = jnp.zeros((inputs, spectra_dev, length), jnp.float32)
    for offset in range(tap_count):
        filtered = (
            filtered + taps[offset][None, None, :] * extended[:, offset : offset + spectra_dev]
        )
    channels = length // 2
    both_parts = transform(filtered.reshape(inputs * spectra_dev, length), length)
    scale = flags.astype(jnp.float32)[None, :, None, None] / (8.0 * math.sqrt(length))
    spectra = (both_parts.reshape(2, inputs, spectra_dev, channels) * scale).astype(jnp.bfloat16)
    turned = lax.all_to_all(
        spectra[:, None], ("inp", "tm"), split_axis=4, concat_axis=1, tiled=True
    )
    groups_inp = lax.axis_size("inp")
    groups_tm = lax.axis_size("tm")
    local_channels = channels // (groups_inp * groups_tm)
    out_groups = local_channels // CH_AVG
    rows = turned.reshape(2, groups_inp, groups_tm, inputs, spectra_dev, out_groups, CH_AVG)
    count = float(groups_tm * spectra_dev * CH_AVG)
    products = jnp.einsum(
        "xatisgk,yctjsgk->gxyaicj",
        rows,
        lax.all_gather(rows, "bl", axis=3, tiled=True),
        preferred_element_type=jnp.float32,
    )
    real_vis = products[:, 0, 0] + products[:, 1, 1]
    imag_vis = products[:, 1, 0] - products[:, 0, 1]
    visibilities = jnp.stack([real_vis, imag_vis]) / count
    return visibilities.reshape(
        2, out_groups, groups_inp, inputs, groups_inp * inputs * lax.axis_size("bl")
    )


def solution(mesh):
    in_specs = (P(("inp", "bl"), "tm"), P(), P(("inp", "bl")))
    out_specs = P(None, ("inp", "tm"), None, "bl", None)
    return jax.shard_map(shards, mesh=mesh, in_specs=in_specs, out_specs=out_specs, check_vma=False)
```

profile of v0, /device:TPU:1, one launch (start us, length us, event | category | flops | bytes accessed | tf_op | source)
XLA Modules:
  0.0 725.3 jit_solution(16236080894492939012)
XLA Ops:
  6.5 5.2 slice_convert_fusion
  11.8 3.1 copy.89
  14.9 1.3 collective-permute-start
  16.2 11.3 %convert_element_type.80 = f32[64,65536]{1,0:T(8,128)} convert(s32[64,65536]{1,0:T(8,128)} %param.3) | non-fusion elementwise | flops 4194304 | bytes 33554432 | tf_op jit(solution)/shard_map/convert_element_type | solution.py:54
  27.5 17.6 %reshape.218 = f32[64,4,16384]{2,1,0:T(4,128)} reshape(f32[64,65536]{1,0:T(8,128)} %convert_element_type.80) | data formatting | bytes 33554432 | tf_op jit(solution)/shard_map/reshape | solution.py:54
  45.4 0.3 sine_negate_fusion
  45.6 0.3 fusion.45
  46.0 0.2 fusion.56
  46.2 107.9 %collective-permute-done = bf16[64,3,16384]{2,0,1:T(8,128)(2,1)} collective-permute-done((bf16[64,3,16384]{2,0,1:T(8,128)(2,1)}, bf16[64,3,16384]{2,0,1:T(8,128)(2,1)}, u32[]{:S(2)}, u32[]{:S(2)}) %collective-permute-start) | collective-permute-done | bytes 6291488 | tf_op jit(solution)/shard_map/ppermute | solution.py:13
  154.1 11.2 %copy.53 = f32[64,3,16384]{2,1,0:T(4,128)} copy(bf16[64,3,16384]{2,0,1:T(8,128)(2,1)} %collective-permute-done) | data formatting | bytes 18874368 | tf_op jit(solution)/shard_map/convert_element_type | solution.py:57
  165.3 32.6 %fusion.8 = f32[64,4,16384]{2,1,0:T(4,128)} fusion(f32[64,4,16384]{2,1,0:T(4,128)S(1)} %copy-done, f32[64,3,16384]{2,1,0:T(4,128)} %copy.53, f32[16384]{0:T(1024)S(1)} %bitcast.77, f32[16384]{0:T(1024)S(1)} %bitcast.78, f32[16384]{0:T(1024)S(1)} %bitcast.76, f32[16384]{0:T(1024)S(1)} %bitcast.75), kind=kLoop, calls=%fused_computation.13 | loop fusion | flops 41943040 | bytes 46399488 | tf_op jit(solution)/shard_map/add | solution.py:61
  197.9 20.5 %reshape_reshape.6 = f32[256,128,128]{2,1,0:T(8,128)} reshape(f32[64,4,16384]{2,1,0:T(4,128)} %fusion.8) | data formatting | bytes 33554432 | tf_op jit(solution)/shard_map/reshape;reshape | solution.py:29
  218.4 32.5 %fusion.17 = f32[256,2,128,128]{2,3,1,0:T(8,128)} fusion(f32[256,128,128]{2,1,0:T(8,128)} %reshape_reshape.6, f32[1,128,128]{2,1,0:T(8,128)S(1)} %get-tuple-element.15, f32[1,128,128]{2,1,0:T(8,128)S(1)} %get-tuple-element.16), kind=kOutput, calls=%fused_computation.26 | convolution fusion | flops 12884934656 | bytes 50462720 | tf_op jit(solution)/shard_map/ykn,mnb->mykb/dot_general | solution.py:32
  250.8 17.8 %multiply_add_fusion = (f32[256,1,128,128]{2,3,1,0:T(8,128)S(1)}, f32[256,1,128,128]{2,3,1,0:T(8,128)}) fusion(f32[256,2,128,128]{2,3,1,0:T(8,128)} %fusion.17, f32[128,128]{0,1:T(8,128)S(1)} %get-tuple-element.17, f32[128,128]{0,1:T(8,128)S(1)} %get-tuple-element.18), kind=kLoop, calls=%fused_computation.25 | loop fusion | flops 25165824 | bytes 67239936 | tf_op jit(solution)/shard_map/add | solution.py:37
  268.6 23.6 %fusion.25 = f32[2,256,64,128]{3,2,1,0:T(8,128)} fusion(f32[256,1,128,128]{2,3,1,0:T(8,128)} %get-tuple-element.6, f32[256,1,128,128]{2,3,1,0:T(8,128)S(1)} %get-tuple-element.5, f32[1,128,2,64]{1,3,0,2:T(8,128)S(1)} %get-tuple-element.14, f32[1,128,2,64]{1,3,0,2:T(8,128)S(1)} %get-tuple-element.13), kind=kOutput, calls=%fused_computation.30 | convolution fusion | flops 12893323264 | bytes 50462720 | tf_op jit(solution)/shard_map/mxkb,xbyq->ymqk/dot_general | solution.py:44
  292.2 19.9 %reshape_reshape.7 = f32[2,1,64,4,8192]{4,3,2,0,1:T(4,128)} reshape(f32[2,256,64,128]{3,2,1,0:T(8,128)} %fusion.25) | data formatting | bytes 33554432 | tf_op jit(solution)/shard_map/reshape;reshape | solution.py:66
  312.2 16.6 %fusion.16 = bf16[2,1,64,4,8192]{4,2,3,1,0:T(8,128)(2,1)} fusion(f32[2,1,64,4,8192]{4,3,2,0,1:T(4,128)} %reshape_reshape.7, f32[64]{0:T(128)S(1)} %convert_multiply_fusion), kind=kLoop, calls=%fused_computation.23 | loop fusion | flops 8388608 | bytes 25166080 | tf_op jit(solution)/shard_map/convert_element_type | solution.py:66
  328.8 24.4 %copy.57 = bf16[2,1,64,4,8192]{2,3,0,1,4:T(4,128)(2,1)} copy(bf16[2,1,64,4,8192]{4,2,3,1,0:T(8,128)(2,1)} %fusion.16) | data formatting | bytes 16777216 | tf_op jit(solution)/shard_map/convert_element_type | solution.py:66
  353.2 26.5 %reshape.228 = bf16[64,2,32768]{2,1,0:T(2,128)(2,1)} reshape(bf16[8192,1,2,4,64]{4,3,2,1,0:T(4,128)(2,1)} %bitcast.68) | data formatting | bytes 16777216
  379.7 108.5 %all_to_all.15 = bf16[64,2,32768]{2,1,0:T(2,128)(2,1)} all-to-all(bf16[64,2,32768]{2,1,0:T(2,128)(2,1)} %reshape.228), channel_id=1, replica_groups=mesh['inp'=8,'tm'=8,'bl'=2] {'inp','tm'}, dimensions={0} | all-to-all | bytes 16777216 | tf_op jit(solution)/shard_map/all_to_all | solution.py:67
  488.2 26.0 %reshape.229 = bf16[8192,1,2,4,64]{4,3,2,1,0:T(4,128)(2,1)} reshape(bf16[64,2,32768]{2,1,0:T(2,128)(2,1)} %all_to_all.15) | data formatting | bytes 16777216
  514.2 23.4 %copy.77 = bf16[2,1,64,4,64,128]{5,2,3,4,0,1:T(8,128)(2,1)} copy(bf16[2,1,64,4,64,128]{2,3,0,5,4,1:T(4,128)(2,1)} %bitcast.69) | data formatting | bytes 16777216 | tf_op jit(solution)/shard_map/all_to_all | solution.py:67
  537.6 27.8 %reshape.219 = bf16[2,8,8,64,4,2,64]{6,5,3,4,2,1,0:T(2,128)(2,1)} reshape(bf16[2,64,1,64,4,128]{5,3,4,1,0,2:T(8,128)(2,1)} %bitcast.71) | data formatting | bytes 16777216 | tf_op jit(solution)/shard_map/reshape | solution.py:74
  565.4 15.2 %copy.60 = bf16[2,8,8,64,4,2,64]{6,3,2,4,1,0,5:T(8,128)(2,1)} copy(bf16[2,8,8,64,4,2,64]{6,5,3,4,2,1,0:T(2,128)(2,1)} %reshape.219) | data formatting | bytes 16777216 | tf_op jit(solution)/shard_map/reshape | solution.py:74
  580.6 54.9 %all-gather.2.cloned.1.call-done = bf16[2,8,8,128,4,2,64]{6,3,2,4,1,0,5:T(8,128)(2,1)} async-done(((bf16[2,8,8,64,4,2,64]{6,3,2,4,1,0,5:T(8,128)(2,1)}), bf16[2,8,8,128,4,2,64]{6,3,2,4,1,0,5:T(8,128)(2,1)}) %all-gather.2.cloned.1.call-update) | async-done | bytes 16777232 | tf_op jit(solution)/shard_map/all_gather | solution.py:79
  635.4 57.3 %fusion.20 = f32[2,2,2,8,64,8,128]{6,4,3,1,5,2,0:T(8,128)} fusion(bf16[2,8,8,64,4,2,64,1,1]{6,5,3,4,2,1,0,8,7:T(2,128)(2,1)} %bitcast.70, bf16[2,8,8,128,4,2,64]{6,3,2,4,1,0,5:T(8,128)(2,1)} %all-gather.2.cloned.1.call-done), kind=kOutput, calls=%fused_computation.29 | convolution fusion | flops 17179869184 | bytes 41943040 | tf_op jit(solution)/shard_map/xatisgk,yctjsgk->gxyaicj/dot_general | solution.py:76
  692.8 10.4 %slice_add_fusion = (f32[2,1,1,8,64,8,128]{6,4,3,1,5,2,0:T(8,128)}, f32[2,1,1,8,64,8,128]{6,4,3,1,5,2,0:T(8,128)S(1)}) fusion(f32[2,2,2,8,64,8,128]{6,4,3,1,5,2,0:T(8,128)} %fusion.20), kind=kLoop, calls=%fused_computation.33 | loop fusion | flops 2097152 | bytes 25165824 | tf_op jit(solution)/shard_map/add | solution.py:82
  703.1 5.5 copy.62
  708.6 1.0 copy.64
  709.6 3.3 copy.63
  712.9 1.0 copy.65
  713.9 4.4 maximum_multiply_fusion
  (12 shorter events, 0.3 us)
Async XLA Ops:
  6.5 628.9 %all-gather.2.cloned.1.call-start = ((), (), s32[]{:S(2)}) async-start(), calls=%async_computation.1 | async-start | bytes 50331648 | tf_op jit(solution)/shard_map/all_gather | solution.py:79
  14.9 139.2 %collective-permute-start = (bf16[64,3,16384]{2,0,1:T(8,128)(2,1)}, bf16[64,3,16384]{2,0,1:T(8,128)(2,1)}, u32[]{:S(2)}, u32[]{:S(2)}) collective-permute-start(bf16[64,3,16384]{2,0,1:T(8,128)(2,1)} %bitcast.67), channel_id=1, source_target_pairs={{2,0},{4,2},{6,4},{8,6},{10,8},{12,10},{14,12},{3,1},{5,3},{7,5},{... | collective-permute-start | bytes 18874376 | tf_op jit(solution)/shard_map/ppermute | solution.py:13
  27.5 18.5 %copy-start.2 = (s32[64]{0:T(128)S(1)}, s32[64]{0:T(128)}, u32[]{:S(2)}) copy-start(s32[64]{0:T(128)} %param.5) | copy-start | bytes 772
  27.5 18.5 %copy-start.1 = (f32[4,16384]{1,0:T(4,128)S(1)}, f32[4,16384]{1,0:T(4,128)}, u32[]{:S(2)}) copy-start(f32[4,16384]{1,0:T(4,128)} %param.4) | copy-start | bytes 786436
  45.1 120.2 %copy-start = (f32[64,4,16384]{2,1,0:T(4,128)S(1)}, f32[64,4,16384]{2,1,0:T(4,128)}, u32[]{:S(2)}) copy-start(f32[64,4,16384]{2,1,0:T(4,128)} %reshape.218) | copy-start | bytes 50331652
Sparse Core Ops, SparseCore 0:
  580.7 54.6 all-gather.1
where the time goes:
time: 737 us; the launch traced here: 725 us
  local copies, waits for them, and re-layouts  227 us (31%)
  waiting for transfers between devices  163 us (22%)
  matrix products  113 us (15%)
  blocking collectives  108 us (15%)
  other arithmetic  99 us (13%)
  between operations  13.7 us (2%)
    all_to_all x1, blocking collectives, shards(): lax.all_to_all(spectra[:, None], ('inp', 'tm'), split_axis=4, concat_axis...  108 us
    ppermute x1, waiting for transfers between devices, passed_along(): lax.ppermute(value, axis, [(source, source + steps) for source in range(i...  108 us
    dot_general x1, matrix products, shards(): jnp.einsum('xatisgk,yctjsgk->gxyaicj', rows, lax.all_gather(rows, 'bl', a...  57.3 us
    all_gather x1, waiting for transfers between devices, shards(): lax.all_gather(rows, 'bl', axis=3, tiled=True)  54.9 us
    unnamed x8, local copies, waits for them, and re-layouts  52.6 us
    reshape x2, local copies, waits for them, and re-layouts, shards(): turned.reshape(2, groups_inp, groups_tm, inputs, spectra_dev, out_groups,...  43 us
    add x1, other arithmetic, shards(): filtered + taps[offset][None, None, :] * extended[:, offset:offset + spec...  32.6 us
    dot_general x1, matrix products, transform(): jnp.einsum('ykn,mnb->mykb', table_one, blocks, precision=highest)  32.5 us
  transfers between devices with their start and end apart: 2, of which 2 were waited for; matrix products, arithmetic and copies ran while one was open for 4% of the time, Pallas kernels for 0%

commit v1 on v0

--- a/solution.py
+++ b/solution.py
@@ -5,6 +5,11 @@
 from jax.sharding import PartitionSpec as P
 
 CH_AVG = 64
+
+
+def all_by_exchange(x, axis, d):
+    sent = jnp.stack([x] * lax.axis_size(axis))
+    return jnp.concatenate(lax.all_to_all(sent, axis, 0, 0), axis=d)
 
 
 def passed_along(value, axis, steps):
@@ -76,7 +81,7 @@
     products = jnp.einsum(
         "xatisgk,yctjsgk->gxyaicj",
         rows,
-        lax.all_gather(rows, "bl", axis=3, tiled=True),
+        all_by_exchange(rows, "bl", 3),
         preferred_element_type=jnp.float32,
     )
     real_vis = products[:, 0, 0] + products[:, 1, 1]

time: 737 us -> 1040 us (1.41)
  local copies, waits for them, and re-layouts: 227 us -> 513 us
  other arithmetic: 99 us -> 159 us
  waiting for transfers between devices: 163 us -> 108 us
  blocking collectives: 108 us -> 143 us
  matrix products: 113 us -> 94.1 us
  between operations: 13.7 us -> 0.57 us
    reshape x0 -> x3, local copies, waits for them, and re-layouts: none -> 203 us  [all_by_exchange(): return jnp.concatenate(lax.all_to_all(sent, axis, 0, 0), axis=d)]
    unnamed x8 -> x10, local copies, waits for them, and re-layouts: 52.6 us -> 123 us
    unnamed x0 -> x1, other arithmetic: none -> 60.3 us
    all_gather x1 -> x0, waiting for transfers between devices: 54.9 us -> none  [shards(): lax.all_gather(rows, 'bl', axis=3, tiled=True)]
    all_to_all x0 -> x1, blocking collectives: none -> 34.8 us  [all_by_exchange(): return jnp.concatenate(lax.all_to_all(sent, axis, 0, 0), axis=d)]
    another operation x0 -> x1, local copies, waits for them, and re-layouts: none -> 27.8 us  [all_by_exchange(): sent = jnp.stack([x] * lax.axis_size(axis))]
    dot_general x1, matrix products: 57.3 us -> 37.8 us  [shards(): jnp.einsum('xatisgk,yctjsgk->gxyaicj', rows, all_by_exchange(rows, 'bl',...]
    reshape x2 -> x1, local copies, waits for them, and re-layouts: 43 us -> 27.8 us  [shards(): turned.reshape(2, groups_inp, groups_tm, inputs, spectra_dev, out_groups,...]
  transfers between devices with their start and end apart: 2 -> 1, of which waited for: 2 -> 1; matrix products, arithmetic and copies ran while one was open for 4% -> 3% of each run, Pallas kernels for 0% -> 0%
where the time goes in v1:
time: 1040 us; the launch traced here: 1020 us
  local copies, waits for them, and re-layouts  513 us (49%)
  other arithmetic  159 us (15%)
  blocking collectives  143 us (14%)
  waiting for transfers between devices  108 us (10%)
  matrix products  94.1 us (9%)
    reshape x3, local copies, waits for them, and re-layouts, all_by_exchange(): return jnp.concatenate(lax.all_to_all(sent, axis, 0, 0), axis=d)  203 us
    unnamed x10, local copies, waits for them, and re-layouts  123 us
    all_to_all x1, blocking collectives, shards(): lax.all_to_all(spectra[:, None], ('inp', 'tm'), split_axis=4, concat_axis...  108 us
    ppermute x1, waiting for transfers between devices, passed_along(): lax.ppermute(value, axis, [(source, source + steps) for source in range(i...  108 us
    unnamed x1, other arithmetic  60.3 us
    dot_general x1, matrix products, shards(): jnp.einsum('xatisgk,yctjsgk->gxyaicj', rows, all_by_exchange(rows, 'bl',...  37.8 us
    all_to_all x1, blocking collectives, all_by_exchange(): return jnp.concatenate(lax.all_to_all(sent, axis, 0, 0), axis=d)  34.8 us
    add x1, other arithmetic, shards(): filtered + taps[offset][None, None, :] * extended[:, offset:offset + spec...  32.6 us
  transfers between devices with their start and end apart: 1, of which 1 were waited for; matrix products, arithmetic and copies ran while one was open for 3% of the time, Pallas kernels for 0%

profile of v1, /device:TPU:1, one launch (start us, length us, event | category | flops | bytes accessed | tf_op | source)
XLA Modules:
  0.0 1018.8 jit_solution(957770780570440682)
XLA Ops:
  0.0 5.2 slice_convert_fusion
  5.2 3.1 copy.94
  9.6 11.3 %convert_element_type.80 = f32[64,65536]{1,0:T(8,128)} convert(s32[64,65536]{1,0:T(8,128)} %param.3) | non-fusion elementwise | flops 4194304 | bytes 33554432 | tf_op jit(solution)/shard_map/convert_element_type | solution.py:59
  20.9 17.6 %reshape.225 = f32[64,4,16384]{2,1,0:T(4,128)} reshape(f32[64,65536]{1,0:T(8,128)} %convert_element_type.80) | data formatting | bytes 33554432 | tf_op jit(solution)/shard_map/reshape | solution.py:59
  39.6 107.9 %collective-permute-done = bf16[64,3,16384]{2,0,1:T(8,128)(2,1)} collective-permute-done((bf16[64,3,16384]{2,0,1:T(8,128)(2,1)}, bf16[64,3,16384]{2,0,1:T(8,128)(2,1)}, u32[]{:S(2)}, u32[]{:S(2)}) %collective-permute-start) | collective-permute-done | bytes 6291488 | tf_op jit(solution)/shard_map/ppermute | solution.py:18
  147.5 11.2 %copy.56 = f32[64,3,16384]{2,1,0:T(4,128)} copy(bf16[64,3,16384]{2,0,1:T(8,128)(2,1)} %collective-permute-done) | data formatting | bytes 18874368 | tf_op jit(solution)/shard_map/convert_element_type | solution.py:62
  158.8 32.6 %fusion.6 = f32[64,4,16384]{2,1,0:T(4,128)} fusion(f32[64,4,16384]{2,1,0:T(4,128)S(1)} %copy-done, f32[64,3,16384]{2,1,0:T(4,128)} %copy.56, f32[16384]{0:T(1024)S(1)} %bitcast.89, f32[16384]{0:T(1024)S(1)} %bitcast.90, f32[16384]{0:T(1024)S(1)} %bitcast.88, f32[16384]{0:T(1024)S(1)} %bitcast.87), kind=kLoop, calls=%fused_computation.12 | loop fusion | flops 41943040 | bytes 46399488 | tf_op jit(solution)/shard_map/add | solution.py:66
  191.4 20.5 %reshape_reshape.6 = f32[256,128,128]{2,1,0:T(8,128)} reshape(f32[64,4,16384]{2,1,0:T(4,128)} %fusion.6) | data formatting | bytes 33554432 | tf_op jit(solution)/shard_map/reshape;reshape | solution.py:34
  211.9 32.5 %fusion.17 = f32[256,2,128,128]{2,3,1,0:T(8,128)} fusion(f32[256,128,128]{2,1,0:T(8,128)} %reshape_reshape.6, f32[1,128,128]{2,1,0:T(8,128)S(1)} %get-tuple-element.15, f32[1,128,128]{2,1,0:T(8,128)S(1)} %get-tuple-element.16), kind=kOutput, calls=%fused_computation.27 | convolution fusion | flops 12884934656 | bytes 50462720 | tf_op jit(solution)/shard_map/ykn,mnb->mykb/dot_general | solution.py:37
  244.4 17.7 %multiply_add_fusion = (f32[256,1,128,128]{2,3,1,0:T(8,128)S(1)}, f32[256,1,128,128]{2,3,1,0:T(8,128)}) fusion(f32[256,2,128,128]{2,3,1,0:T(8,128)} %fusion.17, f32[128,128]{0,1:T(8,128)S(1)} %get-tuple-element.17, f32[128,128]{0,1:T(8,128)S(1)} %get-tuple-element.18), kind=kLoop, calls=%fused_computation.26 | loop fusion | flops 25165824 | bytes 67239936 | tf_op jit(solution)/shard_map/add | solution.py:42
  262.1 23.8 %fusion.25 = f32[2,256,64,128]{3,2,1,0:T(8,128)} fusion(f32[256,1,128,128]{2,3,1,0:T(8,128)} %get-tuple-element.6, f32[256,1,128,128]{2,3,1,0:T(8,128)S(1)} %get-tuple-element.5, f32[1,128,2,64]{1,3,0,2:T(8,128)S(1)} %get-tuple-element.14, f32[1,128,2,64]{1,3,0,2:T(8,128)S(1)} %get-tuple-element.13), kind=kOutput, calls=%fused_computation.31 | convolution fusion | flops 12893323264 | bytes 50462720 | tf_op jit(solution)/shard_map/mxkb,xbyq->ymqk/dot_general | solution.py:49
  285.9 19.9 %reshape_reshape.7 = f32[2,1,64,4,8192]{4,3,2,0,1:T(4,128)} reshape(f32[2,256,64,128]{3,2,1,0:T(8,128)} %fusion.25) | data formatting | bytes 33554432 | tf_op jit(solution)/shard_map/reshape;reshape | solution.py:71
  305.8 16.6 %fusion.16 = bf16[2,1,64,4,8192]{4,2,3,1,0:T(8,128)(2,1)} fusion(f32[2,1,64,4,8192]{4,3,2,0,1:T(4,128)} %reshape_reshape.7, f32[64]{0:T(128)S(1)} %convert_multiply_fusion), kind=kLoop, calls=%fused_computation.24 | loop fusion | flops 8388608 | bytes 25166080 | tf_op jit(solution)/shard_map/convert_element_type | solution.py:71
  322.4 24.4 %copy.60 = bf16[2,1,64,4,8192]{2,3,0,1,4:T(4,128)(2,1)} copy(bf16[2,1,64,4,8192]{4,2,3,1,0:T(8,128)(2,1)} %fusion.16) | data formatting | bytes 16777216 | tf_op jit(solution)/shard_map/convert_element_type | solution.py:71
  346.9 26.5 %reshape.238 = bf16[64,2,32768]{2,1,0:T(2,128)(2,1)} reshape(bf16[8192,1,2,4,64]{4,3,2,1,0:T(4,128)(2,1)} %bitcast.81) | data formatting | bytes 16777216
  373.4 108.2 %all_to_all.20 = bf16[64,2,32768]{2,1,0:T(2,128)(2,1)} all-to-all(bf16[64,2,32768]{2,1,0:T(2,128)(2,1)} %reshape.238), channel_id=1, replica_groups=mesh['inp'=8,'tm'=8,'bl'=2] {'inp','tm'}, dimensions={0} | all-to-all | bytes 16777216 | tf_op jit(solution)/shard_map/all_to_all | solution.py:72
  481.6 26.0 %reshape.239 = bf16[8192,1,2,4,64]{4,3,2,1,0:T(4,128)(2,1)} reshape(bf16[64,2,32768]{2,1,0:T(2,128)(2,1)} %all_to_all.20) | data formatting | bytes 16777216
  507.5 23.4 %copy.81 = bf16[2,1,64,4,64,128]{5,2,3,4,0,1:T(8,128)(2,1)} copy(bf16[2,1,64,4,64,128]{2,3,0,5,4,1:T(4,128)(2,1)} %bitcast.82) | data formatting | bytes 16777216 | tf_op jit(solution)/shard_map/all_to_all | solution.py:72
  530.9 27.8 %stack_reshape.4 = bf16[1,2,8,8,64,4,2,64]{7,6,4,5,3,2,1,0:T(2,128)(2,1)} reshape(bf16[2,64,1,64,4,128]{5,3,4,1,0,2:T(8,128)(2,1)} %bitcast.79) | data formatting | bytes 16777216 | tf_op jit(solution)/shard_map/stack;reshape | solution.py:11
  558.7 27.8 %reshape.228 = bf16[2,8,8,64,4,2,64]{6,5,3,4,2,1,0:T(2,128)(2,1)} reshape(bf16[2,64,1,64,4,128]{5,3,4,1,0,2:T(8,128)(2,1)} %bitcast.80) | data formatting | bytes 16777216 | tf_op jit(solution)/shard_map/reshape | solution.py:79
  586.6 60.3 %fusion.57 = bf16[2,2,8,8,4,64,2,64]{7,6,5,4,3,2,1,0:T(2,128)(2,1)} fusion(bf16[1,2,8,8,64,4,2,64]{7,6,4,5,3,2,1,0:T(2,128)(2,1)} %stack_reshape.4), kind=kLoop, calls=%fused_computation.81 | loop fusion | flops 8388608 | bytes 25165824
  646.8 27.6 %reshape.240 = bf16[2,2,2097152]{2,1,0:T(2,128)(2,1)} reshape(bf16[2,2,8,8,4,64,2,64]{7,6,5,4,3,2,1,0:T(2,128)(2,1)} %fusion.57) | data formatting | bytes 33554432
  674.4 34.8 %all_to_all.21 = bf16[2,2,2097152]{2,1,0:T(2,128)(2,1)} all-to-all(bf16[2,2,2097152]{2,1,0:T(2,128)(2,1)} %reshape.240), channel_id=1, replica_groups=mesh['inp'=8,'tm'=8,'bl'=2] {'bl'}, dimensions={0} | all-to-all | bytes 33554432 | tf_op jit(solution)/shard_map/all_to_all | solution.py:12
  709.2 43.1 %reshape.241 = bf16[2,2,8,8,4,64,2,64]{7,6,5,4,3,2,1,0:T(2,128)(2,1)} reshape(bf16[2,2,2097152]{2,1,0:T(2,128)(2,1)} %all_to_all.21) | data formatting | bytes 33554432
  752.3 28.9 %bitcast_bitcast_fusion = bf16[2,8,8,2,64,4,2,64]{7,6,4,5,2,1,0,3:T(2,128)(2,1)} fusion(bf16[2,2,8,8,4,64,2,64]{7,6,5,4,3,2,1,0:T(2,128)(2,1)} %reshape.241), kind=kLoop, calls=%fused_computation.82 | loop fusion | bytes 33554432 | tf_op jit(solution)/shard_map/reshape | solution.py:12
  781.2 121.3 %copy.63 = bf16[2,8,8,2,64,4,2,64]{4,3,7,2,5,1,0,6:T(2,128)(2,1)} copy(bf16[2,8,8,2,64,4,2,64]{7,6,4,5,2,1,0,3:T(2,128)(2,1)} %bitcast_bitcast_fusion) | data formatting | bytes 33554432 | tf_op jit(solution)/shard_map/reshape | solution.py:12
  902.5 52.4 %reshape.234 = bf16[2,8,8,128,4,2,64,1,1]{3,6,2,4,1,0,5,7,8:T(8,128)(2,1)} reshape(bf16[2,8,8,2,64,4,2,64]{4,3,7,2,5,1,0,6:T(2,128)(2,1)} %copy.63) | data formatting | bytes 33554432 | tf_op jit(solution)/shard_map/reshape | solution.py:12
  955.0 37.8 %fusion.20 = f32[2,2,2,8,64,8,128]{6,4,3,1,5,2,0:T(8,128)} fusion(bf16[2,8,8,64,4,2,64,1,1]{6,5,3,4,2,1,0,8,7:T(2,128)(2,1)} %bitcast.84, bf16[2,8,8,128,4,2,64,1,1]{3,6,2,4,1,0,5,7,8:T(8,128)(2,1)} %reshape.234), kind=kOutput, calls=%fused_computation.30 | convolution fusion | flops 17179869184 | bytes 41943040 | tf_op jit(solution)/shard_map/xatisgk,yctjsgk->gxyaicj/dot_general | solution.py:81
  992.8 10.4 %slice_add_fusion = (f32[2,1,1,8,64,8,128]{6,4,3,1,5,2,0:T(8,128)}, f32[2,1,1,8,64,8,128]{6,4,3,1,5,2,0:T(8,128)S(1)}) fusion(f32[2,2,2,8,64,8,128]{6,4,3,1,5,2,0:T(8,128)} %fusion.20), kind=kLoop, calls=%fused_computation.34 | loop fusion | flops 2097152 | bytes 25165824 | tf_op jit(solution)/shard_map/add | solution.py:87
  1003.1 5.5 copy.66
  1009.6 3.3 copy.67
  1013.9 4.4 maximum_multiply_fusion
  (16 shorter events, 4.3 us)
Async XLA Ops:
  8.4 139.2 %collective-permute-start = (bf16[64,3,16384]{2,0,1:T(8,128)(2,1)}, bf16[64,3,16384]{2,0,1:T(8,128)(2,1)}, u32[]{:S(2)}, u32[]{:S(2)}) collective-permute-start(bf16[64,3,16384]{2,0,1:T(8,128)(2,1)} %bitcast.78), channel_id=1, source_target_pairs={{2,0},{4,2},{6,4},{8,6},{10,8},{12,10},{14,12},{3,1},{5,3},{7,5},{... | collective-permute-start | bytes 18874376 | tf_op jit(solution)/shard_map/ppermute | solution.py:18
  20.9 18.5 %copy-start.2 = (s32[64]{0:T(128)S(1)}, s32[64]{0:T(128)}, u32[]{:S(2)}) copy-start(s32[64]{0:T(128)} %param.5) | copy-start | bytes 772
  20.9 18.5 %copy-start.1 = (f32[4,16384]{1,0:T(4,128)S(1)}, f32[4,16384]{1,0:T(4,128)}, u32[]{:S(2)}) copy-start(f32[4,16384]{1,0:T(4,128)} %param.4) | copy-start | bytes 786436
  38.5 120.2 %copy-start = (f32[64,4,16384]{2,1,0:T(4,128)S(1)}, f32[64,4,16384]{2,1,0:T(4,128)}, u32[]{:S(2)}) copy-start(f32[64,4,16384]{2,1,0:T(4,128)} %reshape.225) | copy-start | bytes 50331652
